TPU v7x, 32 devices: a whole 2x2x4 slice. The times are simulated.
32 devices in a mesh: fx: 4 (over z), fy: 4 (over x, core), fz: 2 (over y).
Axes of the slice: x: 2, y: 2, z: 4, core: 2. Of those that a mesh axis runs over, the one named last changes fastest.
Arguments:
- pressure: float32 [128, 512, 256], P('fx', 'fy', 'fz'), may hold values from -6 to 6
- source: float32 [128, 512, 256], P('fx', 'fy', 'fz'), may hold values from -6 to 6
- diag_shift: float32 [128, 512, 256], P('fx', 'fy', 'fz'), may hold values from 0.1 to 2
- iface_cells: int32 [262144], P(('fx', 'fy', 'fz')), may hold values from 0 to 524287
- iface_coef: float32 [262144], P(('fx', 'fy', 'fz')), may hold values from -6 to 6
- iface_xyz: float32 [3, 262144], P(None, ('fx', 'fy', 'fz')), may hold values from -6 to 6
- node_xyz: float32 [3, 65536], P(None, ('fx', 'fy', 'fz')), may hold values from -6 to 6
- owners: int32 [2048], P(('fx', 'fy', 'fz')), may hold values from 0 to 31, as said below
- node_lists: int32 [65536, 8], P(('fx', 'fy', 'fz')), may hold values from 0 to 1048575
Outputs:
- new_pressure: float32 [128, 512, 256], P('fx', 'fy', 'fz')
- node_loads: float32 [65536], P(('fx', 'fy', 'fz'))
Inputs may be any that keep to these rules, and one draw needn't show every extreme that they name: `owners`: among the 64 tiles of one device, at most 4 have the same owner; one device owns exactly 4 tiles of every device's block; every device owns at least one tile.
All inputs are finite; a program needn't handle non-finite values.
Results may differ from a plain program's by a relative error of at most 0.0003.
Values sent between devices are 32-bit elements; how exact they have to be, the bound alone decides.
A program may use at most 192 MiB of HBM per device.

v0:
```python
import jax
import jax.numpy as jnp
from jax import lax
from jax.sharding import PartitionSpec as P

ITERS = 4
CAP = 4


GAUSS_RATE = 0.5


def extended(cells, sides, width):
    for axis, dim in sides:
        count = lax.axis_size(axis)
        head = lax.slice_in_dim(cells, 0, width, axis=dim)
        tail = lax.slice_in_dim(cells, cells.shape[dim] - width, cells.shape[dim], axis=dim)
        cells = jnp.concatenate(
            [
                lax.ppermute(tail, axis, [(i, (i + 1) % count) for i in range(count)]),
                cells,
                lax.ppermute(head, axis, [((i + 1) % count, i) for i in range(count)]),
            ],
            axis=dim,
        )
    return cells


def face_sweep(field, source, diag_shift):
    edge_x = jnp.stack([field[0], field[-1]], axis=0)
    edge_y = jnp.stack([field[:, 0], field[:, -1]], axis=1)
    edge_z = jnp.stack([field[:, :, 0], field[:, :, -1]], axis=2)
    halo_x = extended(edge_x, (("fx", 0),), 1)
    halo_y = extended(edge_y, (("fy", 1),), 1)
    halo_z = extended(edge_z, (("fz", 2),), 1)
    index_x = lax.broadcasted_iota(jnp.int32, field.shape, 0)
    index_y = lax.broadcasted_iota(jnp.int32, field.shape, 1)
    index_z = lax.broadcasted_iota(jnp.int32, field.shape, 2)
    last_x = field.shape[0] - 1
    last_y = field.shape[1] - 1
    last_z = field.shape[2] - 1
    neighbours = jnp.where(index_x == 0, halo_x[0][None, :, :], jnp.roll(field, 1, 0))
    neighbours = neighbours + jnp.where(
        index_x == last_x, halo_x[3][None, :, :], jnp.roll(field, -1, 0)
    )
    neighbours = neighbours + jnp.where(
        index_y == 0, halo_y[:, 0][:, None, :], jnp.roll(field, 1, 1)
    )
    neighbours = neighbours + jnp.where(
        index_y == last_y, halo_y[:, 3][:, None, :], jnp.roll(field, -1, 1)
    )
    neighbours = neighbours + jnp.where(
        index_z == 0, halo_z[:, :, 0][:, :, None], jnp.roll(field, 1, 2)
    )
    neighbours = neighbours + jnp.where(
        index_z == last_z, halo_z[:, :, 3][:, :, None], jnp.roll(field, -1, 2)
    )
    return (neighbours + source) / (6.0 + diag_shift)


def on_device(
    pressure, source, diag_shift, iface_cells, iface_coef, iface_xyz, node_xyz, owners, node_lists
):
    devices = lax.axis_size(("fx", "fy", "fz"))
    tiles_dev = owners.shape[0]
    tile_width = iface_coef.shape[0] // tiles_dev
    node_count = node_lists.shape[0]
    neigh_count = node_lists.shape[1]
    lane_width = pressure.shape[2]
    row_table = pressure.reshape(-1, lane_width)
    fetched = row_table[iface_cells // lane_width]
    lane_pick = (iface_cells % lane_width)[:, None] == lax.broadcasted_iota(
        jnp.int32, (1, lane_width), 1
    )
    at_cells = jnp.sum(jnp.where(lane_pick, fetched, 0.0), axis=1)
    values = iface_coef * at_cells
    payload = jnp.concatenate(
        [
            values.reshape(tiles_dev, 1, tile_width),
            iface_xyz.reshape(3, tiles_dev, tile_width).transpose(1, 0, 2),
        ],
        axis=1,
    )
    payload = payload.reshape(tiles_dev, 4 * tile_width)
    owned_by = (owners[:, None] == jnp.arange(devices, dtype=jnp.int32)[None, :]).astype(jnp.int32)
    earlier = jnp.cumsum(owned_by, axis=0) - owned_by
    order_rank = jnp.sum(earlier * owned_by, axis=1)
    target = owners * CAP + order_rank
    placing = (target[None, :] == jnp.arange(devices * CAP, dtype=jnp.int32)[:, None]).astype(
        jnp.float32
    )
    outgoing = jnp.dot(
        placing, payload, precision=lax.Precision.HIGHEST, preferred_element_type=jnp.float32
    )
    outgoing = outgoing.reshape(devices * CAP, 4, tile_width)
    filled = jnp.sum(placing, axis=1)
    incoming, arrived = (
        lax.all_to_all(outgoing, ("fx", "fy", "fz"), split_axis=0, concat_axis=0, tiled=True),
        lax.all_to_all(filled, ("fx", "fy", "fz"), split_axis=0, concat_axis=0, tiled=True),
    )
    arrived_int = arrived.astype(jnp.int32)
    prefix = jnp.cumsum(arrived_int)
    owned_count = prefix[-1]
    wanted = (node_lists % owned_count).reshape(node_count * neigh_count)
    selector = ((prefix[None, :] == wanted[:, None] + 1) & (arrived_int[None, :] > 0)).astype(
        jnp.float32
    )
    picked = jnp.dot(
        selector,
        incoming.reshape(devices * CAP, 4 * tile_width),
        precision=lax.Precision.HIGHEST,
        preferred_element_type=jnp.float32,
    )
    picked = picked.reshape(node_count, neigh_count, 4, tile_width)
    distance = jnp.zeros((node_count, neigh_count, tile_width), jnp.float32)
    for component in range(3):
        gap_axis = node_xyz[component][:, None, None] - picked[:, :, component + 1, :]
        distance = distance + gap_axis * gap_axis
    node_loads = jnp.sum(jnp.exp(-GAUSS_RATE * distance) * picked[:, :, 0, :], axis=(1, 2))
    pressure_now = pressure
    for sweep_index in range(ITERS):
        pressure_now = face_sweep(pressure_now, source, diag_shift)
    return (pressure_now, node_loads)


def solution(mesh):
    placed = (
        P("fx", "fy", "fz"),
        P("fx", "fy", "fz"),
        P("fx", "fy", "fz"),
        P(("fx", "fy", "fz")),
        P(("fx", "fy", "fz")),
        P(None, ("fx", "fy", "fz")),
        P(None, ("fx", "fy", "fz")),
        P(("fx", "fy", "fz")),
        P(("fx", "fy", "fz"), None),
    )
    return jax.shard_map(
        on_device,
        mesh=mesh,
        in_specs=placed,
        out_specs=(P("fx", "fy", "fz"), P(("fx", "fy", "fz"))),
        check_vma=False,
    )
```

profile of v0, /device:TPU:0, one launch (start us, length us, event | category | flops | bytes accessed | tf_op | source)
XLA Modules:
  0.0 251.7 jit_solution(13367614697641180582)
XLA Ops:
  0.6 4.9 %fusion.78 = (f32[32,128,1]{2,1,0:T(8,128)}, f32[32,128,1]{2,1,0:T(8,128)}) fusion(f32[32,128,128]{2,1,0:T(8,128)} %param.9), kind=kLoop, calls=%fused_computation.130 | loop fusion | bytes 65536 | tf_op jit(solution)/shard_map/slice | solution.py:32
  7.9 3.0 %collective-permute-start.4 = (f32[32,128,1]{1,0,2:T(8,128)S(1)}, f32[32,128,1]{1,0,2:T(8,128)S(1)}, u32[]{:S(2)}, u32[]{:S(2)}) collective-permute-start(f32[32,128,1]{1,0,2:T(8,128)S(1)} %copy.133), channel_id=1, source_target_pairs={{0,1},{1,0},{2,3},{3,2},{4,5},{5,4},{6,7},{7,6},{8,9},{9,8},{10,11... | collective-permute-start | bytes 49160 | tf_op jit(solution)/shard_map/ppermute | solution.py:20
  18.7 4.5 %all-to-all-start = ((f32[32,4,1]{1,2,0:T(1,128)}), f32[32,4,1]{1,2,0:T(1,128)S(1)}, u32[]{:S(2)}, u32[]{:S(2)}) async-start(f32[32,4,1]{1,2,0:T(1,128)} %bitcast.25), calls=%async_computation | async-start | bytes 32768 | tf_op jit(solution)/shard_map/all_to_all | solution.py:99
  23.2 2.8 %fusion.77 = (f32[32,128,127]{2,1,0:T(8,128)}, f32[32,128,127]{2,1,0:T(8,128)}) fusion(f32[32,128,128]{2,1,0:T(8,128)S(1)} %copy-done), kind=kLoop, calls=%fused_computation.129 | loop fusion | bytes 8323072 | tf_op jit(solution)/shard_map/jit(_roll_static)/slice | solution.py:56
  30.8 27.9 %gather_fusion = f32[8192,128]{1,0:T(8,128)} fusion(f32[4096,128]{1,0:T(8,128)S(1)} %bitcast.112, s32[8192]{0:T(1024)S(1)} %get-tuple-element.60), kind=kCustom, calls=%fused_computation | custom fusion | bytes 8421376 | tf_op jit(solution)/shard_map/gather | solution.py:71
  58.8 4.9 %select_reduce_fusion = f32[8192]{0:T(1024)S(1)} fusion(f32[8192,128]{1,0:T(8,128)} %gather_fusion, s32[8192]{0:T(1024)S(1)} %get-tuple-element.59), kind=kLoop, calls=%fused_computation.21 | loop fusion | flops 3137536 | bytes 4259840 | tf_op jit(solution)/shard_map/reduce_sum | solution.py:75
  85.6 5.8 %all-to-all-start.1 = ((f32[128,4,128]{2,1,0:T(4,128)}), f32[128,4,128]{2,1,0:T(4,128)S(1)}, u32[]{:S(2)}, u32[]{:S(2)}) async-start(f32[128,4,128]{2,1,0:T(4,128)} %copy.118), calls=%async_computation.1 | async-start | bytes 524288 | tf_op jit(solution)/shard_map/all_to_all | solution.py:98
  97.8 11.7 %fusion.25 = f32[32,128,128]{2,0,1:T(8,128)S(1)} fusion(f32[31,128,128]{2,0,1:T(8,128)} %copy.126, f32[1,128,128]{2,0,1:T(1,128)S(1)} %bitcast.117, f32[1,128,128]{2,0,1:T(1,128)S(1)} %bitcast.115, f32[31,128,128]{2,0,1:T(8,128)} %copy.128, f32[32,127,128]{2,0,1:T(8,128)} %copy.130, f32[32,1,128]{2,0,1:T(8,128)S(1)} %bitcast.131, ...), kind=kLoop, calls=%fused_computation.33 | loop fusion | flops 10485760 | bytes 19071296 | tf_op jit(solution)/shard_map/div | solution.py:58
  109.5 2.8 %fusion.72 = (f32[32,128,1]{2,0,1:T(8,128)}, f32[32,128,1]{2,0,1:T(8,128)}) fusion(f32[32,128,128]{2,0,1:T(8,128)S(1)} %fusion.25), kind=kLoop, calls=%fused_computation.124 | loop fusion | bytes 65536 | tf_op jit(solution)/shard_map/slice | solution.py:32
  112.3 2.8 %fusion.71 = (f32[32,128,127]{2,0,1:T(8,128)}, f32[32,128,127]{2,0,1:T(8,128)}) fusion(f32[32,128,128]{2,0,1:T(8,128)S(1)} %fusion.25), kind=kLoop, calls=%fused_computation.123 | loop fusion | bytes 8323072 | tf_op jit(solution)/shard_map/jit(_roll_static)/slice | solution.py:56
  115.1 2.6 %fusion.75 = (f32[31,128,128]{2,0,1:T(8,128)}, f32[31,128,128]{2,0,1:T(8,128)}) fusion(f32[32,128,128]{2,0,1:T(8,128)S(1)} %fusion.25), kind=kLoop, calls=%fused_computation.127 | loop fusion | bytes 8126464 | tf_op jit(solution)/shard_map/jit(_roll_static)/slice | solution.py:44
  117.8 2.7 %copy.99 = f32[32,128,1]{1,0,2:T(8,128)S(1)} copy(f32[32,128,1]{2,0,1:T(8,128)} %get-tuple-element.35) | data formatting | bytes 32768 | tf_op jit(solution)/shard_map/slice | solution.py:32
  121.9 2.7 %copy.101 = f32[32,128,1]{1,0,2:T(8,128)S(1)} copy(f32[32,128,1]{2,0,1:T(8,128)} %get-tuple-element.34) | data formatting | bytes 32768 | tf_op jit(solution)/shard_map/slice | solution.py:32
  130.9 2.7 %fusion.73 = (f32[32,127,128]{2,0,1:T(8,128)}, f32[32,127,128]{2,0,1:T(8,128)}) fusion(f32[32,128,128]{2,0,1:T(8,128)S(1)} %fusion.25), kind=kLoop, calls=%fused_computation.125 | loop fusion | bytes 8323072 | tf_op jit(solution)/shard_map/jit(_roll_static)/slice | solution.py:50
  133.8 11.7 %fusion.32 = f32[32,128,128]{2,0,1:T(8,128)S(1)} fusion(f32[31,128,128]{2,0,1:T(8,128)} %get-tuple-element.41, f32[1,128,128]{2,0,1:T(1,128)S(1)} %get-tuple-element.43, f32[1,128,128]{2,0,1:T(1,128)S(1)} %get-tuple-element.42, f32[31,128,128]{2,0,1:T(8,128)} %get-tuple-element.40, f32[32,127,128]{2,0,1:T(8,128)} %get-tuple-element.37, ...), kind=kLoop, calls=%fused_computation.46 | loop fusion | flops 10485760 | bytes 19071296 | tf_op jit(solution)/shard_map/div | solution.py:58
  145.6 2.8 %fusion.66 = (f32[32,128,1]{2,0,1:T(8,128)}, f32[32,128,1]{2,0,1:T(8,128)}) fusion(f32[32,128,128]{2,0,1:T(8,128)S(1)} %fusion.32), kind=kLoop, calls=%fused_computation.118 | loop fusion | bytes 65536 | tf_op jit(solution)/shard_map/slice | solution.py:32
  148.3 2.8 %fusion.65 = (f32[32,128,127]{2,0,1:T(8,128)}, f32[32,128,127]{2,0,1:T(8,128)}) fusion(f32[32,128,128]{2,0,1:T(8,128)S(1)} %fusion.32), kind=kLoop, calls=%fused_computation.117 | loop fusion | bytes 8323072 | tf_op jit(solution)/shard_map/jit(_roll_static)/slice | solution.py:56
  153.8 2.7 %copy.104 = f32[32,128,1]{1,0,2:T(8,128)S(1)} copy(f32[32,128,1]{2,0,1:T(8,128)} %get-tuple-element.23) | data formatting | bytes 32768 | tf_op jit(solution)/shard_map/slice | solution.py:32
  158.0 2.7 %copy.106 = f32[32,128,1]{1,0,2:T(8,128)S(1)} copy(f32[32,128,1]{2,0,1:T(8,128)} %get-tuple-element.22) | data formatting | bytes 32768 | tf_op jit(solution)/shard_map/slice | solution.py:32
  161.2 3.8 %collective-permute-start.13 = (f32[1,128,128]{2,0,1:T(1,128)S(1)}, f32[1,128,128]{2,0,1:T(1,128)S(1)}, u32[]{:S(2)}, u32[]{:S(2)}) collective-permute-start(f32[1,128,128]{2,0,1:T(1,128)S(1)} %get-tuple-element.30), channel_id=1, source_target_pairs={{8,0},{16,8},{24,16},{0,24},{9,1},{17,9},{25,17},{1,25},{10,2},{18... | collective-permute-start | bytes 196616 | tf_op jit(solution)/shard_map/ppermute | solution.py:22
  167.0 2.7 %fusion.67 = (f32[32,127,128]{2,0,1:T(8,128)}, f32[32,127,128]{2,0,1:T(8,128)}) fusion(f32[32,128,128]{2,0,1:T(8,128)S(1)} %fusion.32), kind=kLoop, calls=%fused_computation.119 | loop fusion | bytes 8323072 | tf_op jit(solution)/shard_map/jit(_roll_static)/slice | solution.py:50
  169.9 11.7 %fusion.39 = f32[32,128,128]{2,0,1:T(8,128)S(1)} fusion(f32[31,128,128]{2,0,1:T(8,128)} %get-tuple-element.29, f32[1,128,128]{2,0,1:T(1,128)S(1)} %get-tuple-element.31, f32[1,128,128]{2,0,1:T(1,128)S(1)} %get-tuple-element.30, f32[31,128,128]{2,0,1:T(8,128)} %get-tuple-element.28, f32[32,127,128]{2,0,1:T(8,128)} %get-tuple-element.25, ...), kind=kLoop, calls=%fused_computation.59 | loop fusion | flops 10485760 | bytes 19071296 | tf_op jit(solution)/shard_map/div | solution.py:58
  181.7 2.8 %fusion.60 = (f32[32,128,1]{2,0,1:T(8,128)}, f32[32,128,1]{2,0,1:T(8,128)}) fusion(f32[32,128,128]{2,0,1:T(8,128)S(1)} %fusion.39), kind=kLoop, calls=%fused_computation.112 | loop fusion | bytes 65536 | tf_op jit(solution)/shard_map/slice | solution.py:32
  184.4 2.6 %fusion.63 = (f32[31,128,128]{2,0,1:T(8,128)}, f32[31,128,128]{2,0,1:T(8,128)}) fusion(f32[32,128,128]{2,0,1:T(8,128)S(1)} %fusion.39), kind=kLoop, calls=%fused_computation.115 | loop fusion | bytes 8126464 | tf_op jit(solution)/shard_map/jit(_roll_static)/slice | solution.py:44
  187.1 2.8 %fusion.59 = (f32[32,128,127]{2,0,1:T(8,128)}, f32[32,128,127]{2,0,1:T(8,128)}) fusion(f32[32,128,128]{2,0,1:T(8,128)S(1)} %fusion.39), kind=kLoop, calls=%fused_computation.111 | loop fusion | bytes 8323072 | tf_op jit(solution)/shard_map/jit(_roll_static)/slice | solution.py:56
  190.0 2.7 %copy.109 = f32[32,128,1]{1,0,2:T(8,128)S(1)} copy(f32[32,128,1]{2,0,1:T(8,128)} %get-tuple-element.11) | data formatting | bytes 32768 | tf_op jit(solution)/shard_map/slice | solution.py:32
  194.1 2.7 %copy.111 = f32[32,128,1]{1,0,2:T(8,128)S(1)} copy(f32[32,128,1]{2,0,1:T(8,128)} %get-tuple-element.10) | data formatting | bytes 32768 | tf_op jit(solution)/shard_map/slice | solution.py:32
  197.4 3.8 %collective-permute-start.19 = (f32[1,128,128]{2,0,1:T(1,128)S(1)}, f32[1,128,128]{2,0,1:T(1,128)S(1)}, u32[]{:S(2)}, u32[]{:S(2)}) collective-permute-start(f32[1,128,128]{2,0,1:T(1,128)S(1)} %get-tuple-element.18), channel_id=1, source_target_pairs={{8,0},{16,8},{24,16},{0,24},{9,1},{17,9},{25,17},{1,25},{10,2},{18... | collective-permute-start | bytes 196616 | tf_op jit(solution)/shard_map/ppermute | solution.py:22
  203.2 2.7 %fusion.61 = (f32[32,127,128]{2,0,1:T(8,128)}, f32[32,127,128]{2,0,1:T(8,128)}) fusion(f32[32,128,128]{2,0,1:T(8,128)S(1)} %fusion.39), kind=kLoop, calls=%fused_computation.113 | loop fusion | bytes 8323072 | tf_op jit(solution)/shard_map/jit(_roll_static)/slice | solution.py:50
  206.1 11.7 %fusion.46 = f32[32,128,128]{2,0,1:T(8,128)S(1)} fusion(f32[31,128,128]{2,0,1:T(8,128)} %get-tuple-element.17, f32[1,128,128]{2,0,1:T(1,128)S(1)} %get-tuple-element.19, f32[1,128,128]{2,0,1:T(1,128)S(1)} %get-tuple-element.18, f32[31,128,128]{2,0,1:T(8,128)} %get-tuple-element.16, f32[32,127,128]{2,0,1:T(8,128)} %get-tuple-element.13, ...), kind=kLoop, calls=%fused_computation.72 | loop fusion | flops 10485760 | bytes 19071296 | tf_op jit(solution)/shard_map/div | solution.py:58
  220.5 17.6 %fusion.12 = f32[2048,8,4,128]{0,3,2,1:T(8,128)} fusion(s32[2048,8]{0,1:T(8,128)S(1)} %fusion.51, s32[128]{0:T(128)S(1)} %reduce.1, pred[128]{0:T(512)(128)(4,1)S(1)} %gt.13, f32[128,4,128]{0,2,1:T(8,128)S(1)} %copy.119), kind=kOutput, calls=%fused_computation.17 | convolution fusion | flops 12889096192 | bytes 33882752 | tf_op jit(solution)/shard_map/dot_general | solution.py:108
  238.1 13.4 %fusion.1 = f32[2048]{0:T(1024)} fusion(f32[2048,8,4,128]{0,3,2,1:T(8,128)} %fusion.12, f32[2048]{0:T(1024)S(1)} %bitcast.133, f32[2048]{0:T(1024)S(1)} %bitcast.134, f32[2048]{0:T(1024)S(1)} %bitcast.132), kind=kLoop, calls=%fused_computation.3 | loop fusion | flops 23066624 | bytes 33587200 | tf_op jit(solution)/shard_map/reduce_sum | solution.py:119
  (130 shorter events, 63.9 us)
Async XLA Ops:
  5.6 7.6 %copy-start = (f32[32,128,128]{2,1,0:T(8,128)S(1)}, f32[32,128,128]{2,1,0:T(8,128)}, u32[]{:S(2)}) copy-start(f32[32,128,128]{2,1,0:T(8,128)} %param.9) | copy-start | bytes 6291460
  5.6 12.0 %copy-start.14 = (s32[64]{0:T(128)S(1)}, s32[64]{0:T(128)}, u32[]{:S(2)}) copy-start(s32[64]{0:T(128)} %param.16) | copy-start | bytes 772
  7.9 86.3 %collective-permute-start.4 = (f32[32,128,1]{1,0,2:T(8,128)S(1)}, f32[32,128,1]{1,0,2:T(8,128)S(1)}, u32[]{:S(2)}, u32[]{:S(2)}) collective-permute-start(f32[32,128,1]{1,0,2:T(8,128)S(1)} %copy.133), channel_id=1, source_target_pairs={{0,1},{1,0},{2,3},{3,2},{4,5},{5,4},{6,7},{7,6},{8,9},{9,8},{10,11... | collective-permute-start | bytes 49160 | tf_op jit(solution)/shard_map/ppermute | solution.py:20
  13.2 83.6 %collective-permute-start.5 = (f32[32,128,1]{1,0,2:T(8,128)S(1)}, f32[32,128,1]{1,0,2:T(8,128)S(1)}, u32[]{:S(2)}, u32[]{:S(2)}) collective-permute-start(f32[32,128,1]{1,0,2:T(8,128)S(1)} %copy.135), channel_id=1, source_target_pairs={{1,0},{0,1},{3,2},{2,3},{5,4},{4,5},{7,6},{6,7},{9,8},{8,9},{11,10... | collective-permute-start | bytes 49160 | tf_op jit(solution)/shard_map/ppermute | solution.py:22
  13.2 84.5 %collective-permute-start = (f32[1,128,128]{2,0,1:T(1,128)S(1)}, f32[1,128,128]{2,0,1:T(1,128)S(1)}, u32[]{:S(2)}, u32[]{:S(2)}) collective-permute-start(f32[1,128,128]{2,0,1:T(1,128)S(1)} %bitcast.116), channel_id=1, source_target_pairs={{0,8},{8,16},{16,24},{24,0},{1,9},{9,17},{17,25},{25,1},{2,10},{10... | collective-permute-start | bytes 196616 | tf_op jit(solution)/shard_map/ppermute | solution.py:20
  15.4 82.4 %collective-permute-start.1 = (f32[1,128,128]{2,0,1:T(1,128)S(1)}, f32[1,128,128]{2,0,1:T(1,128)S(1)}, u32[]{:S(2)}, u32[]{:S(2)}) collective-permute-start(f32[1,128,128]{2,0,1:T(1,128)S(1)} %bitcast.114), channel_id=1, source_target_pairs={{8,0},{16,8},{24,16},{0,24},{9,1},{17,9},{25,17},{1,25},{10,2},{18... | collective-permute-start | bytes 196616 | tf_op jit(solution)/shard_map/ppermute | solution.py:22
  17.5 79.4 %collective-permute-start.2 = (f32[32,1,128]{2,0,1:T(8,128)S(1)}, f32[32,1,128]{2,0,1:T(8,128)S(1)}, u32[]{:S(2)}, u32[]{:S(2)}) collective-permute-start(f32[32,1,128]{2,0,1:T(8,128)S(1)} %bitcast.130), channel_id=1, source_target_pairs={{0,2},{2,4},{4,6},{6,0},{1,3},{3,5},{5,7},{7,1},{8,10},{10,12},{12... | collective-permute-start | bytes 49160 | tf_op jit(solution)/shard_map/ppermute | solution.py:20
  18.7 66.9 %all-to-all-start = ((f32[32,4,1]{1,2,0:T(1,128)}), f32[32,4,1]{1,2,0:T(1,128)S(1)}, u32[]{:S(2)}, u32[]{:S(2)}) async-start(f32[32,4,1]{1,2,0:T(1,128)} %bitcast.25), calls=%async_computation | async-start | bytes 32768 | tf_op jit(solution)/shard_map/all_to_all | solution.py:99
  58.7 4.9 %copy-start.9 = (f32[3,8192]{1,0:T(4,128)S(1)}, f32[3,8192]{1,0:T(4,128)}, u32[]{:S(2)}) copy-start(f32[3,8192]{1,0:T(4,128)} %param.14) | copy-start | bytes 294916
  58.7 5.4 %copy-start.13 = (f32[3,2048]{1,0:T(4,128)S(1)}, f32[3,2048]{1,0:T(4,128)}, u32[]{:S(2)}) copy-start(f32[3,2048]{1,0:T(4,128)} %param.15) | copy-start | bytes 73732
  58.8 5.4 %copy-start.2 = (f32[32,128,1]{2,1,0:T(8,128)S(1)}, f32[32,128,1]{2,1,0:T(8,128)}, u32[]{:S(2)}) copy-start(f32[32,128,1]{2,1,0:T(8,128)} %get-tuple-element.47) | copy-start | bytes 49156
  82.1 11.4 %copy-start.10 = (s32[2048,8]{0,1:T(8,128)S(1)}, s32[2048,8]{0,1:T(8,128)}, u32[]{:S(2)}) copy-start(s32[2048,8]{0,1:T(8,128)} %param.17) | copy-start | bytes 196612
  85.6 134.8 %all-to-all-start.1 = ((f32[128,4,128]{2,1,0:T(4,128)}), f32[128,4,128]{2,1,0:T(4,128)S(1)}, u32[]{:S(2)}, u32[]{:S(2)}) async-start(f32[128,4,128]{2,1,0:T(4,128)} %copy.118), calls=%async_computation.1 | async-start | bytes 524288 | tf_op jit(solution)/shard_map/all_to_all | solution.py:98
  94.3 3.5 %collective-permute-start.3 = (f32[32,1,128]{2,0,1:T(8,128)S(1)}, f32[32,1,128]{2,0,1:T(8,128)S(1)}, u32[]{:S(2)}, u32[]{:S(2)}) collective-permute-start(f32[32,1,128]{2,0,1:T(8,128)S(1)} %bitcast.128), channel_id=1, source_target_pairs={{2,0},{4,2},{6,4},{0,6},{3,1},{5,3},{7,5},{1,7},{10,8},{12,10},{14... | collective-permute-start | bytes 49160 | tf_op jit(solution)/shard_map/ppermute | solution.py:22
  120.4 8.6 %collective-permute-start.10 = (f32[32,128,1]{1,0,2:T(8,128)S(1)}, f32[32,128,1]{1,0,2:T(8,128)S(1)}, u32[]{:S(2)}, u32[]{:S(2)}) collective-permute-start(f32[32,128,1]{1,0,2:T(8,128)S(1)} %copy.99), channel_id=1, source_target_pairs={{0,1},{1,0},{2,3},{3,2},{4,5},{5,4},{6,7},{7,6},{8,9},{9,8},{10,11... | collective-permute-start | bytes 49160 | tf_op jit(solution)/shard_map/ppermute | solution.py:20
  124.6 9.1 %collective-permute-start.11 = (f32[32,128,1]{1,0,2:T(8,128)S(1)}, f32[32,128,1]{1,0,2:T(8,128)S(1)}, u32[]{:S(2)}, u32[]{:S(2)}) collective-permute-start(f32[32,128,1]{1,0,2:T(8,128)S(1)} %copy.101), channel_id=1, source_target_pairs={{1,0},{0,1},{3,2},{2,3},{5,4},{4,5},{7,6},{6,7},{9,8},{8,9},{11,10... | collective-permute-start | bytes 49160 | tf_op jit(solution)/shard_map/ppermute | solution.py:22
  125.2 8.6 %collective-permute-start.6 = (f32[1,128,128]{2,0,1:T(1,128)S(1)}, f32[1,128,128]{2,0,1:T(1,128)S(1)}, u32[]{:S(2)}, u32[]{:S(2)}) collective-permute-start(f32[1,128,128]{2,0,1:T(1,128)S(1)} %get-tuple-element.43), channel_id=1, source_target_pairs={{0,8},{8,16},{16,24},{24,0},{1,9},{9,17},{17,25},{25,1},{2,10},{10... | collective-permute-start | bytes 196616 | tf_op jit(solution)/shard_map/ppermute | solution.py:20
  126.6 7.2 %collective-permute-start.7 = (f32[1,128,128]{2,0,1:T(1,128)S(1)}, f32[1,128,128]{2,0,1:T(1,128)S(1)}, u32[]{:S(2)}, u32[]{:S(2)}) collective-permute-start(f32[1,128,128]{2,0,1:T(1,128)S(1)} %get-tuple-element.42), channel_id=1, source_target_pairs={{8,0},{16,8},{24,16},{0,24},{9,1},{17,9},{25,17},{1,25},{10,2},{18... | collective-permute-start | bytes 196616 | tf_op jit(solution)/shard_map/ppermute | solution.py:22
  129.0 4.8 %collective-permute-start.8 = (f32[32,1,128]{2,0,1:T(8,128)S(1)}, f32[32,1,128]{2,0,1:T(8,128)S(1)}, u32[]{:S(2)}, u32[]{:S(2)}) collective-permute-start(f32[32,1,128]{2,0,1:T(8,128)S(1)} %get-tuple-element.39), channel_id=1, source_target_pairs={{0,2},{2,4},{4,6},{6,0},{1,3},{3,5},{5,7},{7,1},{8,10},{10,12},{12... | collective-permute-start | bytes 49160 | tf_op jit(solution)/shard_map/ppermute | solution.py:20
  129.0 4.8 %collective-permute-start.9 = (f32[32,1,128]{2,0,1:T(8,128)S(1)}, f32[32,1,128]{2,0,1:T(8,128)S(1)}, u32[]{:S(2)}, u32[]{:S(2)}) collective-permute-start(f32[32,1,128]{2,0,1:T(8,128)S(1)} %get-tuple-element.38), channel_id=1, source_target_pairs={{2,0},{4,2},{6,4},{0,6},{3,1},{5,3},{7,5},{1,7},{10,8},{12,10},{14... | collective-permute-start | bytes 49160 | tf_op jit(solution)/shard_map/ppermute | solution.py:22
  156.5 8.6 %collective-permute-start.16 = (f32[32,128,1]{1,0,2:T(8,128)S(1)}, f32[32,128,1]{1,0,2:T(8,128)S(1)}, u32[]{:S(2)}, u32[]{:S(2)}) collective-permute-start(f32[32,128,1]{1,0,2:T(8,128)S(1)} %copy.104), channel_id=1, source_target_pairs={{0,1},{1,0},{2,3},{3,2},{4,5},{5,4},{6,7},{7,6},{8,9},{9,8},{10,11... | collective-permute-start | bytes 49160 | tf_op jit(solution)/shard_map/ppermute | solution.py:20
  160.6 9.2 %collective-permute-start.17 = (f32[32,128,1]{1,0,2:T(8,128)S(1)}, f32[32,128,1]{1,0,2:T(8,128)S(1)}, u32[]{:S(2)}, u32[]{:S(2)}) collective-permute-start(f32[32,128,1]{1,0,2:T(8,128)S(1)} %copy.106), channel_id=1, source_target_pairs={{1,0},{0,1},{3,2},{2,3},{5,4},{4,5},{7,6},{6,7},{9,8},{8,9},{11,10... | collective-permute-start | bytes 49160 | tf_op jit(solution)/shard_map/ppermute | solution.py:22
  161.2 8.7 %collective-permute-start.12 = (f32[1,128,128]{2,0,1:T(1,128)S(1)}, f32[1,128,128]{2,0,1:T(1,128)S(1)}, u32[]{:S(2)}, u32[]{:S(2)}) collective-permute-start(f32[1,128,128]{2,0,1:T(1,128)S(1)} %get-tuple-element.31), channel_id=1, source_target_pairs={{0,8},{8,16},{16,24},{24,0},{1,9},{9,17},{17,25},{25,1},{2,10},{10... | collective-permute-start | bytes 196616 | tf_op jit(solution)/shard_map/ppermute | solution.py:20
  161.2 8.7 %collective-permute-start.13 = (f32[1,128,128]{2,0,1:T(1,128)S(1)}, f32[1,128,128]{2,0,1:T(1,128)S(1)}, u32[]{:S(2)}, u32[]{:S(2)}) collective-permute-start(f32[1,128,128]{2,0,1:T(1,128)S(1)} %get-tuple-element.30), channel_id=1, source_target_pairs={{8,0},{16,8},{24,16},{0,24},{9,1},{17,9},{25,17},{1,25},{10,2},{18... | collective-permute-start | bytes 196616 | tf_op jit(solution)/shard_map/ppermute | solution.py:22
  165.1 4.8 %collective-permute-start.14 = (f32[32,1,128]{2,0,1:T(8,128)S(1)}, f32[32,1,128]{2,0,1:T(8,128)S(1)}, u32[]{:S(2)}, u32[]{:S(2)}) collective-permute-start(f32[32,1,128]{2,0,1:T(8,128)S(1)} %get-tuple-element.27), channel_id=1, source_target_pairs={{0,2},{2,4},{4,6},{6,0},{1,3},{3,5},{5,7},{7,1},{8,10},{10,12},{12... | collective-permute-start | bytes 49160 | tf_op jit(solution)/shard_map/ppermute | solution.py:20
  165.1 4.8 %collective-permute-start.15 = (f32[32,1,128]{2,0,1:T(8,128)S(1)}, f32[32,1,128]{2,0,1:T(8,128)S(1)}, u32[]{:S(2)}, u32[]{:S(2)}) collective-permute-start(f32[32,1,128]{2,0,1:T(8,128)S(1)} %get-tuple-element.26), channel_id=1, source_target_pairs={{2,0},{4,2},{6,4},{0,6},{3,1},{5,3},{7,5},{1,7},{10,8},{12,10},{14... | collective-permute-start | bytes 49160 | tf_op jit(solution)/shard_map/ppermute | solution.py:22
  192.6 8.6 %collective-permute-start.22 = (f32[32,128,1]{1,0,2:T(8,128)S(1)}, f32[32,128,1]{1,0,2:T(8,128)S(1)}, u32[]{:S(2)}, u32[]{:S(2)}) collective-permute-start(f32[32,128,1]{1,0,2:T(8,128)S(1)} %copy.109), channel_id=1, source_target_pairs={{0,1},{1,0},{2,3},{3,2},{4,5},{5,4},{6,7},{7,6},{8,9},{9,8},{10,11... | collective-permute-start | bytes 49160 | tf_op jit(solution)/shard_map/ppermute | solution.py:20
  196.8 9.2 %collective-permute-start.23 = (f32[32,128,1]{1,0,2:T(8,128)S(1)}, f32[32,128,1]{1,0,2:T(8,128)S(1)}, u32[]{:S(2)}, u32[]{:S(2)}) collective-permute-start(f32[32,128,1]{1,0,2:T(8,128)S(1)} %copy.111), channel_id=1, source_target_pairs={{1,0},{0,1},{3,2},{2,3},{5,4},{4,5},{7,6},{6,7},{9,8},{8,9},{11,10... | collective-permute-start | bytes 49160 | tf_op jit(solution)/shard_map/ppermute | solution.py:22
  197.4 8.7 %collective-permute-start.18 = (f32[1,128,128]{2,0,1:T(1,128)S(1)}, f32[1,128,128]{2,0,1:T(1,128)S(1)}, u32[]{:S(2)}, u32[]{:S(2)}) collective-permute-start(f32[1,128,128]{2,0,1:T(1,128)S(1)} %get-tuple-element.19), channel_id=1, source_target_pairs={{0,8},{8,16},{16,24},{24,0},{1,9},{9,17},{17,25},{25,1},{2,10},{10... | collective-permute-start | bytes 196616 | tf_op jit(solution)/shard_map/ppermute | solution.py:20
  197.4 8.7 %collective-permute-start.19 = (f32[1,128,128]{2,0,1:T(1,128)S(1)}, f32[1,128,128]{2,0,1:T(1,128)S(1)}, u32[]{:S(2)}, u32[]{:S(2)}) collective-permute-start(f32[1,128,128]{2,0,1:T(1,128)S(1)} %get-tuple-element.18), channel_id=1, source_target_pairs={{8,0},{16,8},{24,16},{0,24},{9,1},{17,9},{25,17},{1,25},{10,2},{18... | collective-permute-start | bytes 196616 | tf_op jit(solution)/shard_map/ppermute | solution.py:22
  201.2 4.9 %collective-permute-start.20 = (f32[32,1,128]{2,0,1:T(8,128)S(1)}, f32[32,1,128]{2,0,1:T(8,128)S(1)}, u32[]{:S(2)}, u32[]{:S(2)}) collective-permute-start(f32[32,1,128]{2,0,1:T(8,128)S(1)} %get-tuple-element.15), channel_id=1, source_target_pairs={{0,2},{2,4},{4,6},{6,0},{1,3},{3,5},{5,7},{7,1},{8,10},{10,12},{12... | collective-permute-start | bytes 49160 | tf_op jit(solution)/shard_map/ppermute | solution.py:20
  201.2 4.9 %collective-permute-start.21 = (f32[32,1,128]{2,0,1:T(8,128)S(1)}, f32[32,1,128]{2,0,1:T(8,128)S(1)}, u32[]{:S(2)}, u32[]{:S(2)}) collective-permute-start(f32[32,1,128]{2,0,1:T(8,128)S(1)} %get-tuple-element.14), channel_id=1, source_target_pairs={{2,0},{4,2},{6,4},{0,6},{3,1},{5,3},{7,5},{1,7},{10,8},{12,10},{14... | collective-permute-start | bytes 49160 | tf_op jit(solution)/shard_map/ppermute | solution.py:22
  (9 other events, 25.3 us)
where the time goes:
time: 256 us; the launch traced here: 252 us
  local copies, waits for them, and re-layouts  120 us (47%)
  other arithmetic  66.8 us (26%)
  starting transfers between devices  43.3 us (17%)
  matrix products  18 us (7%)
  between operations  2.62 us (1%)
    div x4, other arithmetic, face_sweep(): return (neighbours + source) / (6.0 + diag_shift)  46.8 us
    slice x12, local copies, waits for them, and re-layouts, face_sweep(): edge_z = jnp.stack([field[:, :, 0], field[:, :, -1]], axis=2)  34.3 us
    gather x1, local copies, waits for them, and re-layouts, on_device(): fetched = row_table[iface_cells // lane_width]  27.9 us
    unnamed x39, local copies, waits for them, and re-layouts  22.5 us
    ppermute x12, starting transfers between devices, extended(): lax.ppermute(head, axis, [((i + 1) % count, i) for i in range(count)])  21.8 us
    dot_general x1, matrix products, on_device(): jnp.dot(selector, incoming.reshape(devices * CAP, 4 * tile_width), precis...  17.6 us
    reduce_sum x1, other arithmetic, on_device(): jnp.sum(jnp.exp(-GAUSS_RATE * distance) * picked[:, :, 0, :], axis=(1, 2))  13.4 us
    ppermute x12, starting transfers between devices, extended(): lax.ppermute(tail, axis, [(i, (i + 1) % count) for i in range(count)])  11.2 us
  transfers between devices with their start and end apart: 26, of which 1 were waited for; matrix products, arithmetic and copies ran while one was open for 66% of the time, Pallas kernels for 0%

commit v1 on v0

v1 whole, which is shorter than its diff:
```python
import functools
import math

import jax
import jax.numpy as jnp
from jax import lax
from jax.experimental import pallas as pl
from jax.experimental.pallas import tpu as pltpu
from jax.sharding import PartitionSpec as P

ITERS = 4
CAP = 4
GAUSS_RATE = 0.5
SCALE = math.sqrt(GAUSS_RATE * math.log2(math.e))
FAR = 1.0e6
NODE_BLOCK = 256
MESH = pl.DeviceIdType.MESH
F32 = jnp.float32
BF16 = jnp.bfloat16


def split2(x):
    hi = x.astype(BF16)
    return hi, (x - hi.astype(F32)).astype(BF16)


def split3(x):
    hi = x.astype(BF16)
    rest = x - hi.astype(F32)
    mid = rest.astype(BF16)
    return hi, mid, (rest - mid.astype(F32)).astype(BF16)


def mm(a, b):
    return jnp.dot(a, b, preferred_element_type=F32)


def iota(shape, dim):
    return lax.broadcasted_iota(jnp.int32, shape, dim)


def ones_where(mask):
    return jnp.where(mask, 1.0, 0.0).astype(BF16)


def route_kernel(
    devices, cells_s, table, cells, coef, xyz, owners, out, rows, parts
):
    tiles, width = cells.shape
    lanes = table.shape[1]
    shift = lanes.bit_length() - 1

    def fetch(t, carry):
        base = t * width
        for p in range(width):
            at = lax.shift_right_logical(cells_s[base + p], shift)
            rows[pl.ds(base + p, 1), :] = table[pl.ds(at, 1), :]
        return carry

    lax.fori_loop(0, tiles, fetch, 0)

    diagonal = iota((width, width), 0) == iota((width, width), 1)

    def pick(t, carry):
        base = pl.multiple_of(t * width, width)
        hi, lo = split2(rows[pl.ds(base, width), :])
        lane = jnp.bitwise_and(cells[pl.ds(t, 1), :], lanes - 1)
        chosen = ones_where(iota((lanes, width), 0) == lane)
        got = mm(hi, chosen) + mm(lo, chosen)
        got = jnp.sum(jnp.where(diagonal, got, 0.0), axis=0, keepdims=True)
        parts[3, pl.ds(t, 1), :] = got * coef[pl.ds(t, 1), :]
        for c in range(3):
            parts[c, pl.ds(t, 1), :] = xyz[c : c + 1, pl.ds(base, width)]
        return carry

    lax.fori_loop(0, tiles, pick, 0, unroll=2)

    own = owners[...]
    mine = iota((devices, tiles), 0) == own
    before = ones_where(iota((tiles, tiles), 0) < iota((tiles, tiles), 1))
    earlier = mm(ones_where(mine), before)
    rank = jnp.sum(jnp.where(mine, earlier, 0.0), axis=0, keepdims=True)
    target = own * CAP + rank.astype(jnp.int32)
    line = iota((devices * 8, tiles), 0)
    at_slot = (line // 8) * CAP + line % CAP == target
    low = line % 8 < CAP
    first = ones_where(at_slot & low)
    second = ones_where(at_slot & jnp.logical_not(low))
    filled = mm(first, jnp.ones((tiles, width), BF16))
    for half in range(2):
        total = None
        for sel, c in ((first, 2 * half), (second, 2 * half + 1)):
            for piece in split3(parts[c]):
                term = mm(sel, piece)
                total = term if total is None else total + term
        if half == 0:
            empty = (iota(filled.shape, 0) % 8 < CAP) & (filled < 0.5)
            total = jnp.where(empty, FAR, total)
        out[half] = total.reshape(devices, 8, width)


def main_kernel(
    sizes,
    p_any, s_any, d_any, outgoing, nodes, lists,
    new_p, loads,
    a_buf, b_buf, src, inv, hx, hy, hz, ys, zs, incoming, tab, pos, want,
    load_sem, x_send, x_recv, y_send, y_recv, z_send, z_recv, t_send, t_recv,
):
    nfx, nfy, nfz = sizes
    devices = nfx * nfy * nfz
    cx, cy, cz = src.shape
    width = outgoing.shape[-1]
    bx, by, bz = lax.axis_index("fx"), lax.axis_index("fy"), lax.axis_index("fz")
    me = (bx * nfy + by) * nfz + bz
    pad = 8
    body = pl.ds(pad, cy)

    load_p = pltpu.make_async_copy(p_any, a_buf.at[:, body, :], load_sem.at[0])
    load_s = pltpu.make_async_copy(s_any, src, load_sem.at[1])
    load_d = pltpu.make_async_copy(d_any, inv, load_sem.at[2])
    load_p.start()
    load_s.start()
    load_d.start()

    def coords(flat):
        return (flat // (nfy * nfz), (flat // nfz) % nfy, flat % nfz)

    barrier = pltpu.get_barrier_semaphore()

    def greet(o, carry):
        pl.semaphore_signal(
            barrier, inc=1, device_id=coords((me + o) % devices), device_id_type=MESH
        )
        return carry

    lax.fori_loop(1, devices, greet, 0)
    pl.semaphore_wait(barrier, devices - 1)

    def remote(a, b, ss, rs, device):
        return pltpu.make_async_remote_copy(
            src_ref=a, dst_ref=b, send_sem=ss, recv_sem=rs, device_id=device, device_id_type=MESH
        )

    def tile_copy(o):
        to = (me + o) % devices
        return remote(
            outgoing.at[:, to], incoming.at[:, me], t_send.at[o], t_recv.at[o], coords(to)
        )

    x_next, x_prev = ((bx + 1) % nfx, by, bz), ((bx + nfx - 1) % nfx, by, bz)
    y_next, y_prev = (bx, (by + 1) % nfy, bz), (bx, (by + nfy - 1) % nfy, bz)
    z_next, z_prev = (bx, by, (bz + 1) % nfz), (bx, by, (bz + nfz - 1) % nfz)

    def x_copies(it, buf):
        return [
            remote(buf.at[cx - 1, body], hx.at[it, 0], x_send.at[it, 0], x_recv.at[it, 0], x_next),
            remote(buf.at[0, body], hx.at[it, 1], x_send.at[it, 1], x_recv.at[it, 1], x_prev),
        ]

    def yz_copies(it):
        made = [
            remote(ys.at[it, 1], hy.at[it, 0], y_send.at[it, 0], y_recv.at[it, 0], y_next),
            remote(ys.at[it, 0], hy.at[it, 1], y_send.at[it, 1], y_recv.at[it, 1], y_prev),
            remote(zs.at[it], hz.at[it, 0], z_send.at[it, 0], z_recv.at[it, 0], z_next),
        ]
        if nfz > 2:
            made.append(
                remote(zs.at[it], hz.at[it, 1], z_send.at[it, 1], z_recv.at[it, 1], z_prev)
            )
        return made

    lane = iota((cy, cz), 1)
    pair = lax.shift_right_logical(lane, 1)

    def faces(it, x, plane, packed):
        ys[it, 0, pl.ds(x, 1), :] = plane[0:1]
        ys[it, 1, pl.ds(x, 1), :] = plane[cy - 1 : cy]
        return jnp.where(pair == x, pltpu.roll(plane, 2 * x + 1, 1), packed)

    load_p.wait()
    started = [x_copies(0, a_buf)]
    for c in started[0]:
        c.start()

    def first_faces(x, packed):
        return faces(0, x, a_buf[x, pl.ds(pad, cy), :], packed)

    zs[0] = lax.fori_loop(0, cx, first_faces, jnp.zeros((cy, cz), F32))
    started[0] = started[0] + yz_copies(0)
    for c in started[0][2:]:
        c.start()

    def send_tile(o, carry):
        tile_copy(o).start()
        return carry

    lax.fori_loop(1, devices, send_tile, 0)
    incoming[:, me] = outgoing[:, me]
    load_s.wait()
    load_d.wait()

    def sweep(it, cur, nxt):
        last = it == ITERS - 1
        for c in started[it]:
            c.wait_recv()
        if it > 0:
            for c in started[it - 1][:2]:
                c.wait_send()

        def rows(x, carry):
            cur[x, pl.ds(pad - 1, 1), :] = hy[it, 0, pl.ds(x, 1), :]
            cur[x, pl.ds(pad + cy, 1), :] = hy[it, 1, pl.ds(x, 1), :]
            return carry

        lax.fori_loop(0, cx, rows, 0, unroll=4)
        if nfz > 2:
            hz[it, 0] = jnp.where(lane % 2 == 0, hz[it, 0], hz[it, 1])

        def plane(x, below, above, packed):
            mid = cur[x, pl.ds(pad, cy), :]
            edge = pltpu.roll(hz[it, 0], cz - 1 - 2 * x, 1)
            total = pltpu.roll(jnp.where(lane == 0, edge, mid), cz - 1, 1)
            total = total + pltpu.roll(jnp.where(lane == cz - 1, edge, mid), 1, 1)
            total = total + cur[x, pl.ds(pad - 1, cy), :]
            total = total + cur[x, pl.ds(pad + 1, cy), :]
            total = total + below + above + src[x]
            if it == 0:
                scale = 1.0 / (6.0 + inv[x])
                inv[x] = scale
            else:
                scale = inv[x]
            new = total * scale
            if last:
                new_p[x] = new
                return packed
            nxt[x, pl.ds(pad, cy), :] = new
            return faces(it + 1, x, new, packed)

        def at(x):
            return cur[x, pl.ds(pad, cy), :]

        packed = jnp.zeros((cy, cz), F32) if not last else jnp.int32(0)
        packed = plane(0, hx[it, 0], at(1), packed)
        packed = plane(cx - 1, at(cx - 2), hx[it, 1], packed)
        if not last:
            started.append(x_copies(it + 1, nxt))
            for c in started[-1]:
                c.start()
        packed = lax.fori_loop(
            1, cx - 1, lambda x, z: plane(x, at(x - 1), at(x + 1), z), packed
        )
        if not last:
            zs[it + 1] = packed
            more = yz_copies(it + 1)
            for c in more:
                c.start()
            started[-1] = started[-1] + more

    slots = devices * CAP
    lines = devices * 8

    def prepare():
        def wait_tile(o, carry):
            tile_copy(o).wait_recv()
            return carry

        lax.fori_loop(1, devices, wait_tile, 0)
        low = incoming[0].reshape(lines, width)
        high = incoming[1].reshape(lines, width)
        row = iota((lines, slots), 0)
        col = iota((lines, slots), 1)
        home = (row // 8) * CAP + row % CAP
        lower = row % 8 < CAP
        take = (ones_where((home == col) & lower), ones_where((home == col) & (row % 8 >= CAP)))
        for half, block in ((0, low), (1, high)):
            turned = block.T
            for second in range(2):
                c = 2 * half + second
                scaled = turned if c == 3 else turned * SCALE
                hi, lo = split2(scaled)
                tab[c * width : (c + 1) * width, 0:slots] = mm(hi, take[second]).astype(BF16)
                tab[c * width : (c + 1) * width, slots : 2 * slots] = mm(lo, take[second]).astype(
                    BF16
                )
        here = ones_where(low < 0.5 * FAR)
        row = iota((slots, lines), 0)
        col = iota((slots, lines), 1)
        home = (col // 8) * CAP + col % CAP
        lower = col % 8 < CAP
        prefix = mm(ones_where((home <= row) & lower), here)
        there = mm(ones_where((home == row) & lower), here)
        place = jnp.where(there > 0.5, prefix - 1.0, -1.0)
        pos[:, 0:width] = place
        pos[:, width : 2 * width] = place
        count = prefix[slots - 1 : slots, 0:1]
        entry = lists[...].astype(F32)
        rest = entry - jnp.floor(entry / count) * count
        rest = jnp.where(rest < 0.0, rest + count, rest)
        want[...] = jnp.where(rest >= count, rest - count, rest)

    neigh = lists.shape[0]

    def gauss(block, carry):
        span = pl.ds(pl.multiple_of(block * NODE_BLOCK, NODE_BLOCK), NODE_BLOCK)
        here = [nodes[c : c + 1, span] * SCALE for c in range(3)]
        total = jnp.zeros((8, NODE_BLOCK), F32)
        for k in range(neigh):
            hot = ones_where(pos[...] == want[k : k + 1, span])
            hot = jnp.concatenate([hot, hot], axis=0)
            got = mm(tab[...], hot)
            far = None
            for c in range(3):
                gap = got[c * width : (c + 1) * width] - here[c]
                far = gap * gap if far is None else far + gap * gap
            term = jnp.exp2(-far) * got[3 * width : 4 * width]
            total = total + jnp.sum(term.reshape(width // 8, 8, NODE_BLOCK), axis=0)
        loads[:, span] = jnp.sum(total, axis=0, keepdims=True)
        return carry

    blocks = nodes.shape[1] // NODE_BLOCK
    bounds = [blocks * i // (ITERS - 1) for i in range(ITERS)]
    bufs = (a_buf, b_buf)
    for it in range(ITERS):
        sweep(it, bufs[it % 2], bufs[(it + 1) % 2])
        if it == 0:
            prepare()
        if it < ITERS - 1:
            lax.fori_loop(bounds[it], bounds[it + 1], gauss, 0)

    for it, group in enumerate(started):
        for c in group if it == ITERS - 1 else group[2:]:
            c.wait_send()

    def drain(o, carry):
        tile_copy(o).wait_send()
        return carry

    lax.fori_loop(1, devices, drain, 0)


def on_device(
    sizes,
    pressure, source, diag_shift, iface_cells, iface_coef, iface_xyz, node_xyz, owners, node_lists,
):
    nfx, nfy, nfz = sizes
    devices = nfx * nfy * nfz
    tiles = owners.shape[0]
    width = iface_coef.shape[0] // tiles
    cx, cy, cz = pressure.shape
    nodes, neigh = node_lists.shape
    vmem = pl.BlockSpec(memory_space=pltpu.VMEM)
    smem = pl.BlockSpec(memory_space=pltpu.SMEM)
    hbm = pl.BlockSpec(memory_space=pl.ANY)
    slots = devices * CAP
    outgoing = pl.pallas_call(
        functools.partial(route_kernel, devices),
        out_shape=jax.ShapeDtypeStruct((2, devices, 8, width), F32),
        in_specs=[smem] + [vmem] * 5,
        out_specs=vmem,
        scratch_shapes=[
            pltpu.VMEM((tiles * width, cz), F32),
            pltpu.VMEM((4, tiles, width), F32),
        ],
        compiler_params=pltpu.CompilerParams(vmem_limit_bytes=48 * 1024 * 1024),
        name="route",
    )(
        iface_cells,
        pressure.reshape(cx * cy, cz),
        iface_cells.reshape(tiles, width),
        iface_coef.reshape(tiles, width),
        iface_xyz,
        owners.reshape(1, tiles),
    )
    dma = pltpu.SemaphoreType.DMA
    new_p, loads = pl.pallas_call(
        functools.partial(main_kernel, sizes),
        out_shape=(
            jax.ShapeDtypeStruct((cx, cy, cz), F32),
            jax.ShapeDtypeStruct((1, nodes), F32),
        ),
        in_specs=[hbm] * 3 + [vmem] * 3,
        out_specs=(vmem, vmem),
        scratch_shapes=[
            pltpu.VMEM((cx, cy + 16, cz), F32),
            pltpu.VMEM((cx, cy + 16, cz), F32),
            pltpu.VMEM((cx, cy, cz), F32),
            pltpu.VMEM((cx, cy, cz), F32),
            pltpu.VMEM((ITERS, 2, cy, cz), F32),
            pltpu.VMEM((ITERS, 2, cx, cz), F32),
            pltpu.VMEM((ITERS, 2, cy, cz), F32),
            pltpu.VMEM((ITERS, 2, cx, cz), F32),
            pltpu.VMEM((ITERS, cy, cz), F32),
            pltpu.VMEM((2, devices, 8, width), F32),
            pltpu.VMEM((4 * width, 2 * slots), BF16),
            pltpu.VMEM((slots, NODE_BLOCK), F32),
            pltpu.VMEM((neigh, nodes), F32),
            dma((3,)),
            dma((ITERS, 2)), dma((ITERS, 2)),
            dma((ITERS, 2)), dma((ITERS, 2)),
            dma((ITERS, 2)), dma((ITERS, 2)),
            dma((devices,)), dma((devices,)),
        ],
        compiler_params=pltpu.CompilerParams(
            collective_id=0, has_side_effects=True, vmem_limit_bytes=56 * 1024 * 1024
        ),
        name="sweeps",
    )(pressure, source, diag_shift, outgoing, node_xyz, node_lists.T)
    return new_p, loads.reshape(nodes)


def solution(mesh):
    sizes = tuple(mesh.shape[a] for a in ("fx", "fy", "fz"))
    cells = P("fx", "fy", "fz")
    flat = P(("fx", "fy", "fz"))
    return jax.shard_map(
        functools.partial(on_device, sizes),
        mesh=mesh,
        in_specs=(
            cells, cells, cells, flat, flat,
            P(None, ("fx", "fy", "fz")), P(None, ("fx", "fy", "fz")), flat,
            P(("fx", "fy", "fz"), None),
        ),
        out_specs=(cells, flat),
        check_vma=False,
    )
```

time: 256 us -> 85.2 us (0.33); the launches traced: 252 us -> 84.9 us
  local copies, waits for them, and re-layouts: 120 us -> 9.1 us
  Pallas kernels: 0 us -> 75.1 us
  other arithmetic: 66.8 us -> 0 us
  starting transfers between devices: 43.3 us -> 0 us
  matrix products: 18 us -> 0 us
    pallas_call x0 -> x2, Pallas kernels: none -> 75.1 us  [the longest x1 58.5 us: on_device(): pl.pallas_call(functools.partial(main_kernel, sizes), out_shape=(jax.Shap...]
    slice x34 -> x0, local copies, waits for them, and re-layouts: 67.1 us -> none  [the longest x12 34.3 us: face_sweep(): edge_z = jnp.stack([field[:, :, 0], field[:, :, -1]], axis=2)]
    div x4 -> x0, other arithmetic: 46.8 us -> none  [face_sweep(): return (neighbours + source) / (6.0 + diag_shift)]
    ppermute x24 -> x0, starting transfers between devices: 33 us -> none  [the longest x12 21.8 us: extended(): lax.ppermute(head, axis, [((i + 1) % count, i) for i in range(count)])]
    gather x1 -> x0, local copies, waits for them, and re-layouts: 27.9 us -> none  [on_device(): fetched = row_table[iface_cells // lane_width]]
    reduce_sum x4 -> x0, other arithmetic: 18.5 us -> none  [the longest x1 13.4 us: on_device(): jnp.sum(jnp.exp(-GAUSS_RATE * distance) * picked[:, :, 0, :], axis=(1, 2))]
    dot_general x2 -> x0, matrix products: 18 us -> none  [the longest x1 17.6 us: on_device(): jnp.dot(selector, incoming.reshape(devices * CAP, 4 * tile_width), precis...]
    unnamed x39 -> x16, local copies, waits for them, and re-layouts: 22.5 us -> 9.1 us
  transfers between devices with their start and end apart: 26 -> 0, of which waited for: 1 -> 0; matrix products, arithmetic and copies ran while one was open for 66% -> 0% of each run, Pallas kernels for 0% -> 0%
where the time goes in v1:
time: 85.2 us; the launch traced here: 84.9 us
  Pallas kernels  75.1 us (88%)
  local copies, waits for them, and re-layouts  9.1 us (11%)
    pallas_call x1, Pallas kernels, on_device(): pl.pallas_call(functools.partial(main_kernel, sizes), out_shape=(jax.Shap...  58.5 us
    pallas_call x1, Pallas kernels, on_device(): pl.pallas_call(functools.partial(route_kernel, devices), out_shape=jax.Sh...  16.5 us
    unnamed x16, local copies, waits for them, and re-layouts  9.1 us

profile of v1, /device:TPU:0, one launch (start us, length us, event | category | flops | bytes accessed | tf_op | source)
XLA Modules:
  0.0 84.9 jit_solution(12126539303349706140)
XLA Ops:
  0.6 0.0 copy-start
  0.6 1.6 %copy-done = f32[32,128,128]{2,1,0:T(8,128)S(1)} copy-done((f32[32,128,128]{2,1,0:T(8,128)S(1)}, f32[32,128,128]{2,1,0:T(8,128)}, u32[]{:S(2)}) %copy-start) | copy-done | bytes 2097176
  2.2 0.0 copy-start.2
  2.2 0.8 copy-done.2
  3.0 0.0 copy-start.3
  3.0 0.9 %copy-done.3 = f32[3,8192]{1,0:T(4,128)S(1)} copy-done((f32[3,8192]{1,0:T(4,128)S(1)}, f32[3,8192]{1,0:T(4,128)}, u32[]{:S(2)}) %copy-start.3) | copy-done | bytes 98328
  3.9 0.0 copy-start.4
  3.9 0.8 copy-done.4
  4.6 0.0 copy-start.5
  4.6 0.7 copy-done.5
  5.3 16.5 %route.1.outgoing = f32[2,32,8,128]{3,2,1,0:T(8,128)S(1)} custom-call(s32[8192]{0:T(1024)S(1)} %copy-done.2, f32[4096,128]{1,0:T(8,128)S(1)} %bitcast.6, s32[64,128]{1,0:T(8,128)S(1)} %bitcast.7, f32[64,128]{1,0:T(8,128)S(1)} %bitcast.8, f32[3,8192]{1,0:T(4,128)S(1)} %copy-done.3, s32[1,64]{1,0:T(1,128)S(1)} %bitcast.9), custom_call_target="tpu_custom_call" | custom-call | tf_op jit(solution)/shard_map/route/pallas_call | solution.py:355
  21.9 0.0 copy-start.1
  21.9 0.7 copy-done.1
  22.6 58.5 %sweeps.1 = (f32[32,128,128]{2,1,0:T(8,128)}, f32[1,2048]{1,0:T(1,128)}) custom-call(f32[32,128,128]{2,1,0:T(8,128)} %p_any.1, f32[32,128,128]{2,1,0:T(8,128)} %s_any.1, f32[32,128,128]{2,1,0:T(8,128)} %d_any.1, f32[2,32,8,128]{3,2,1,0:T(8,128)} %copy-done.1, f32[3,2048]{1,0:T(4,128)} %nodes.1, s32[8,2048]{1,0:T(8,128)} %bitcast.10), custom_call_target="tpu_custom_call" | custom-call | tf_op jit(solution)/shard_map/sweeps/pallas_call | solution.py:375
  81.1 0.0 copy-start.6
  81.1 3.1 %copy.13 = f32[32,128,128]{2,1,0:T(8,128)} copy(f32[32,128,128]{2,1,0:T(8,128)} %get-tuple-element.8) | data formatting | bytes 4194304
  84.3 0.0 copy-done.6
  84.3 0.6 copy.14
Async XLA Ops:
  0.6 1.6 %copy-start = (f32[32,128,128]{2,1,0:T(8,128)S(1)}, f32[32,128,128]{2,1,0:T(8,128)}, u32[]{:S(2)}) copy-start(f32[32,128,128]{2,1,0:T(8,128)} %p_any.1) | copy-start | bytes 6291460
  2.2 0.8 copy-start.2
  3.0 0.9 %copy-start.3 = (f32[3,8192]{1,0:T(4,128)S(1)}, f32[3,8192]{1,0:T(4,128)}, u32[]{:S(2)}) copy-start(f32[3,8192]{1,0:T(4,128)} %xyz.1) | copy-start | bytes 294916
  3.9 0.8 copy-start.4
  4.6 0.7 copy-start.5
  21.9 0.7 copy-start.1
  81.1 3.2 %copy-start.6 = (f32[1,2048]{1,0:T(1,128)S(1)}, f32[1,2048]{1,0:T(1,128)}, u32[]{:S(2)}) copy-start(f32[1,2048]{1,0:T(1,128)} %get-tuple-element.5) | copy-start | bytes 24580
